TPU v7x, 512 devices: a whole 4x4x16 slice. The times are simulated.
512 devices in a mesh: row: 32 (over z_hi, x, core), col: 16 (over y, z_lo).
Axes of the slice: x: 4, y: 4, z: 16 (z_hi: 4, z_lo: 4; z = z_hi * 4 + z_lo), core: 2. Of those that a mesh axis runs over, the one named last changes fastest.
Arguments:
- adjoint: bfloat16 [3, 128, 256, 512], P(None, 'col', 'row'), may hold values from -6 to 6
- velocity: bfloat16 [3, 128, 256, 512], P(None, 'col', 'row'), may hold values from -6 to 6
- control: bfloat16 [256, 512], P('row'), may hold values from -6 to 6
- deriv_x: bfloat16 [2, 512, 512], replicated, may hold values from -0.25 to 0.25
- deriv_y: bfloat16 [2, 256, 256], replicated, may hold values from -0.375 to 0.375
- deriv_z: bfloat16 [2, 128, 128], replicated, may hold values from -0.5 to 0.5
Outputs:
- adjoint_rate: bfloat16 [3, 128, 256, 512], P(None, 'col', 'row')
- control_grad: float32 [256, 512], P('row')
All inputs are finite; a program needn't handle non-finite values.
Results may differ from a plain program's by a relative error of at most 0.009.
Values may be sent and summed in bfloat16 or wider, within the bound.
A program may use at most 64 MiB of HBM per device.

v0:
```python
import jax
import jax.numpy as jnp
from jax import lax
from jax.sharding import PartitionSpec as P


def directional(adjoint_in, velocity_in, matrices, component, grid_dim):
    letters = "abcd"
    source = letters[:grid_dim] + "p" + letters[grid_dim + 1 :]
    target = "m" + letters[:grid_dim] + "q" + letters[grid_dim + 1 :]
    stacked = jnp.einsum(
        source + ",mpq->" + target, adjoint_in, matrices, preferred_element_type=jnp.float32
    )
    deriv_term = stacked[0]
    visc_term = stacked[1]
    speeds = velocity_in.astype(jnp.float32)
    summed = visc_term - speeds[component] * deriv_term
    summed = summed.at[component].add(-jnp.sum(speeds * deriv_term, axis=0))
    return summed.astype(jnp.bfloat16)


def on_device(adjoint, velocity, control, deriv_x, deriv_y, deriv_z):
    part_x = directional(adjoint, velocity, deriv_x, 0, 3)
    span_local = jnp.sum(adjoint[0].astype(jnp.float32) * velocity[0].astype(jnp.float32), axis=0)
    control_grad = lax.psum(span_local, "col")
    normal_adj, normal_vel = (
        lax.all_to_all(adjoint, "row", split_axis=3, concat_axis=2, tiled=True),
        lax.all_to_all(velocity, "row", split_axis=3, concat_axis=2, tiled=True),
    )
    part_y = directional(normal_adj, normal_vel, deriv_y, 1, 2)
    span_part = directional(
        lax.all_to_all(normal_adj, "col", split_axis=2, concat_axis=1, tiled=True),
        lax.all_to_all(normal_vel, "col", split_axis=2, concat_axis=1, tiled=True),
        deriv_z,
        2,
        1,
    )
    back_span = lax.all_to_all(span_part, "col", split_axis=1, concat_axis=2, tiled=True)
    side_normal = (part_y.astype(jnp.float32) + back_span.astype(jnp.float32)).astype(jnp.bfloat16)
    side_sum = lax.all_to_all(side_normal, "row", split_axis=2, concat_axis=3, tiled=True)
    summed = part_x.astype(jnp.float32) + side_sum.astype(jnp.float32)
    forcing = control.astype(jnp.float32)[None] * adjoint[0].astype(jnp.float32)
    summed = summed.at[0].add(forcing)
    return (summed.astype(jnp.bfloat16), control_grad)


def solution(mesh):
    in_specs = (
        P(None, "col", "row", None),
        P(None, "col", "row", None),
        P("row", None),
        P(),
        P(),
        P(),
    )
    out_specs = (P(None, "col", "row", None), P("row", None))
    return jax.shard_map(
        on_device, mesh=mesh, in_specs=in_specs, out_specs=out_specs, check_vma=False
    )
```

profile of v0, /device:TPU:4, one launch (start us, length us, event | category | flops | bytes accessed | tf_op | source)
XLA Modules:
  0.0 268.3 jit_solution(13649834393603836144)
XLA Ops:
  0.6 4.4 %copy.52 = bf16[3,8,8,512]{2,1,0,3:T(8,128)(2,1)} copy(bf16[3,8,8,512]{3,2,1,0:T(8,128)(2,1)} %param.15) | data formatting | bytes 393216 | tf_op args[1]
  5.0 5.6 %reshape.186 = bf16[32,2,1536]{2,1,0:T(2,128)(2,1)} reshape(bf16[512,3,8,8]{3,2,1,0:T(8,128)(2,1)} %bitcast.130) | data formatting | bytes 393216
  10.7 18.2 %all-to-all-start.1 = ((bf16[32,2,1536]{2,1,0:T(2,128)(2,1)}), bf16[32,2,1536]{2,1,0:T(2,128)(2,1)S(1)}, u32[]{:S(2)}, u32[]{:S(2)}) async-start(bf16[32,2,1536]{2,1,0:T(2,128)(2,1)} %reshape.186), calls=%async_computation.1 | async-start | bytes 393216 | tf_op jit(solution)/shard_map/all_to_all | solution.py:28
  28.9 3.5 %copy.48 = bf16[3,8,8,512]{2,1,0,3:T(8,128)(2,1)} copy(bf16[3,8,8,512]{3,2,1,0:T(8,128)(2,1)S(1)} %copy-done.2) | data formatting | bytes 393216 | tf_op args[0]
  32.4 5.6 %reshape.182 = bf16[32,2,1536]{2,1,0:T(2,128)(2,1)} reshape(bf16[512,3,8,8]{3,2,1,0:T(8,128)(2,1)} %bitcast.131) | data formatting | bytes 393216
  38.0 8.4 %all-to-all-done.1 = bf16[32,2,1536]{2,1,0:T(2,128)(2,1)S(1)} async-done(((bf16[32,2,1536]{2,1,0:T(2,128)(2,1)}), bf16[32,2,1536]{2,1,0:T(2,128)(2,1)S(1)}, u32[]{:S(2)}, u32[]{:S(2)}) %all-to-all-start.1) | async-done | bytes 196640 | tf_op jit(solution)/shard_map/all_to_all | solution.py:28
  46.4 7.2 %all-to-all-start = ((bf16[32,2,1536]{2,1,0:T(2,128)(2,1)}), bf16[32,2,1536]{2,1,0:T(2,128)(2,1)S(1)}, u32[]{:S(2)}, u32[]{:S(2)}) async-start(bf16[32,2,1536]{2,1,0:T(2,128)(2,1)} %reshape.182), calls=%async_computation | async-start | bytes 393216 | tf_op jit(solution)/shard_map/all_to_all | solution.py:27
  53.6 4.8 %reshape.187 = bf16[512,3,8,8]{3,2,1,0:T(8,128)(2,1)} reshape(bf16[32,2,1536]{2,1,0:T(2,128)(2,1)S(1)} %all-to-all-done.1) | data formatting | bytes 393216
  58.4 4.0 %copy.80 = bf16[3,8,32,8,16]{4,1,0,3,2:T(8,128)(2,1)S(1)} copy(bf16[3,8,32,8,16]{3,1,0,4,2:T(8,128)(2,1)} %bitcast.122) | data formatting | bytes 393216 | tf_op jit(solution)/shard_map/all_to_all | solution.py:28
  62.4 2.3 reshape.188
  64.7 6.3 %all-to-all-done = bf16[32,2,1536]{2,1,0:T(2,128)(2,1)S(1)} async-done(((bf16[32,2,1536]{2,1,0:T(2,128)(2,1)}), bf16[32,2,1536]{2,1,0:T(2,128)(2,1)S(1)}, u32[]{:S(2)}, u32[]{:S(2)}) %all-to-all-start) | async-done | bytes 196640 | tf_op jit(solution)/shard_map/all_to_all | solution.py:27
  71.0 7.4 %all-to-all-start.3 = ((bf16[16,2,3072]{2,1,0:T(2,128)(2,1)}), bf16[16,2,3072]{2,1,0:T(2,128)(2,1)S(1)}, u32[]{:S(2)}, u32[]{:S(2)}) async-start(bf16[16,2,3072]{2,1,0:T(2,128)(2,1)} %reshape.188), calls=%async_computation.3 | async-start | bytes 393216 | tf_op jit(solution)/shard_map/all_to_all | solution.py:33
  78.4 4.8 %reshape.183 = bf16[512,3,8,8]{3,2,1,0:T(8,128)(2,1)} reshape(bf16[32,2,1536]{2,1,0:T(2,128)(2,1)S(1)} %all-to-all-done) | data formatting | bytes 393216
  83.2 4.0 %copy.79 = bf16[3,8,32,8,16]{4,1,0,3,2:T(8,128)(2,1)S(1)} copy(bf16[3,8,32,8,16]{3,1,0,4,2:T(8,128)(2,1)} %bitcast.124) | data formatting | bytes 393216 | tf_op jit(solution)/shard_map/all_to_all | solution.py:27
  87.2 2.3 reshape.184
  89.5 7.5 %all-to-all-start.2 = ((bf16[16,2,3072]{2,1,0:T(2,128)(2,1)}), bf16[16,2,3072]{2,1,0:T(2,128)(2,1)S(1)}, u32[]{:S(2)}, u32[]{:S(2)}) async-start(bf16[16,2,3072]{2,1,0:T(2,128)(2,1)} %reshape.184), calls=%async_computation.2 | async-start | bytes 393216 | tf_op jit(solution)/shard_map/all_to_all | solution.py:32
  97.1 4.8 %copy.50 = bf16[3,8,32,8,16]{4,3,2,1,0:T(8,128)(2,1)} copy(bf16[3,8,32,8,16]{3,1,0,4,2:T(8,128)(2,1)} %bitcast.125) | data formatting | bytes 393216 | tf_op jit(solution)/shard_map/all_to_all | solution.py:27
  105.2 2.1 copy.82
  111.9 2.3 copy.62
  117.5 2.3 reshape.190
  119.8 7.6 %all-to-all-start.4 = ((bf16[16,2,3072]{2,1,0:T(2,128)(2,1)}), bf16[16,2,3072]{2,1,0:T(2,128)(2,1)}, u32[]{:S(2)}, u32[]{:S(2)}) async-start(bf16[16,2,3072]{2,1,0:T(2,128)(2,1)} %reshape.190), calls=%async_computation.4 | async-start | bytes 393216 | tf_op jit(solution)/shard_map/all_to_all | solution.py:38
  127.4 2.9 %fusion.2 = f32[2,3,8,256,16]{3,4,2,1,0:T(8,128)} fusion(bf16[3,8,32,8,16]{4,3,2,1,0:T(8,128)(2,1)} %copy.50, bf16[2,256,256]{2,1,0:T(8,128)(2,1)S(1)} %copy-done.6), kind=kOutput, calls=%fused_computation.3 | convolution fusion | flops 100663296 | bytes 1245184 | tf_op jit(solution)/shard_map/abpd,mpq->mabqd/dot_general | solution.py:11
  130.3 3.9 %copy.54 = bf16[3,8,32,8,16]{4,3,2,1,0:T(8,128)(2,1)S(1)} copy(bf16[3,8,32,8,16]{3,1,0,4,2:T(8,128)(2,1)} %bitcast.123) | data formatting | bytes 393216 | tf_op jit(solution)/shard_map/all_to_all | solution.py:28
  136.2 2.3 reshape.191
  140.8 3.7 %copy.65 = f32[3,8,16,16,16]{3,2,4,1,0:T(8,128)} copy(f32[3,8,16,16,16]{4,3,1,2,0:T(8,128)} %convert_bitcast_fusion) | data formatting | bytes 786432 | tf_op jit(solution)/shard_map/convert_element_type | solution.py:39
  144.5 2.8 %reshape.171 = f32[3,8,256,16]{2,3,1,0:T(8,128)S(1)} reshape(f32[3,8,16,16,16]{3,2,4,1,0:T(8,128)} %copy.65) | data formatting | bytes 786432 | tf_op jit(solution)/shard_map/convert_element_type | solution.py:39
  148.3 2.4 reshape.192
  150.7 6.8 %all-to-all-start.5 = ((bf16[32,2,1536]{2,1,0:T(2,128)(2,1)}), bf16[32,2,1536]{2,1,0:T(2,128)(2,1)S(1)}, u32[]{:S(2)}, u32[]{:S(2)}) async-start(bf16[32,2,1536]{2,1,0:T(2,128)(2,1)} %reshape.192), calls=%async_computation.5 | async-start | bytes 393216 | tf_op jit(solution)/shard_map/all_to_all | solution.py:40
  158.1 19.1 %all-to-all-done.5 = bf16[32,2,1536]{2,1,0:T(2,128)(2,1)S(1)} async-done(((bf16[32,2,1536]{2,1,0:T(2,128)(2,1)}), bf16[32,2,1536]{2,1,0:T(2,128)(2,1)S(1)}, u32[]{:S(2)}, u32[]{:S(2)}) %all-to-all-start.5) | async-done | bytes 196640 | tf_op jit(solution)/shard_map/all_to_all | solution.py:40
  181.2 4.1 %copy.69 = f32[3,8,8,32,16]{4,3,2,1,0:T(8,128)} copy(f32[3,8,8,32,16]{4,2,3,1,0:T(8,128)} %bitcast.129) | data formatting | bytes 786432 | tf_op jit(solution)/shard_map/convert_element_type | solution.py:41
  185.3 3.6 %reshape.172 = f32[3,8,8,512]{3,2,1,0:T(8,128)S(1)} reshape(f32[3,8,8,32,16]{4,3,2,1,0:T(8,128)} %copy.69) | data formatting | bytes 786432 | tf_op jit(solution)/shard_map/convert_element_type | solution.py:41
  189.9 77.7 %psum.7 = f32[8,512]{1,0:T(8,128)} all-reduce(f32[8,512]{1,0:T(8,128)S(1)} %get-tuple-element.56), channel_id=1, replica_groups=mesh['row'=32,'col'=16] {'col'}, use_global_device_ids=true, to_apply=%region_4.0 | all-reduce | flops 4096 | bytes 32768 | tf_op jit(solution)/shard_map/psum | solution.py:25
  (50 shorter events, 22.5 us)
Async XLA Ops:
  0.6 156.9 %copy-start = (bf16[2,512,512]{2,1,0:T(8,128)(2,1)S(1)}, bf16[2,512,512]{2,1,0:T(8,128)(2,1)}, u32[]{:S(2)}) copy-start(bf16[2,512,512]{2,1,0:T(8,128)(2,1)} %param.17) | copy-start | bytes 3145732
  5.0 23.9 %copy-start.2 = (bf16[3,8,8,512]{3,2,1,0:T(8,128)(2,1)S(1)}, bf16[3,8,8,512]{3,2,1,0:T(8,128)(2,1)}, u32[]{:S(2)}) copy-start(bf16[3,8,8,512]{3,2,1,0:T(8,128)(2,1)} %param.14) | copy-start | bytes 589828
  10.7 35.7 %all-to-all-start.1 = ((bf16[32,2,1536]{2,1,0:T(2,128)(2,1)}), bf16[32,2,1536]{2,1,0:T(2,128)(2,1)S(1)}, u32[]{:S(2)}, u32[]{:S(2)}) async-start(bf16[32,2,1536]{2,1,0:T(2,128)(2,1)} %reshape.186), calls=%async_computation.1 | async-start | bytes 393216 | tf_op jit(solution)/shard_map/all_to_all | solution.py:28
  46.4 24.6 %all-to-all-start = ((bf16[32,2,1536]{2,1,0:T(2,128)(2,1)}), bf16[32,2,1536]{2,1,0:T(2,128)(2,1)S(1)}, u32[]{:S(2)}, u32[]{:S(2)}) async-start(bf16[32,2,1536]{2,1,0:T(2,128)(2,1)} %reshape.182), calls=%async_computation | async-start | bytes 393216 | tf_op jit(solution)/shard_map/all_to_all | solution.py:27
  71.0 18.5 %all-to-all-start.3 = ((bf16[16,2,3072]{2,1,0:T(2,128)(2,1)}), bf16[16,2,3072]{2,1,0:T(2,128)(2,1)S(1)}, u32[]{:S(2)}, u32[]{:S(2)}) async-start(bf16[16,2,3072]{2,1,0:T(2,128)(2,1)} %reshape.188), calls=%async_computation.3 | async-start | bytes 393216 | tf_op jit(solution)/shard_map/all_to_all | solution.py:33
  87.2 9.9 %copy-start.1 = (bf16[3,8,8,512]{3,2,1,0:T(8,128)(2,1)S(1)}, bf16[3,8,8,512]{3,2,1,0:T(8,128)(2,1)}, u32[]{:S(2)}) copy-start(bf16[3,8,8,512]{3,2,1,0:T(8,128)(2,1)} %param.15) | copy-start | bytes 589828
  87.2 9.9 %copy-start.5 = (bf16[8,512]{1,0:T(8,128)(2,1)S(1)}, bf16[8,512]{1,0:T(8,128)(2,1)}, u32[]{:S(2)}) copy-start(bf16[8,512]{1,0:T(8,128)(2,1)} %param.16) | copy-start | bytes 24580
  89.5 17.8 %all-to-all-start.2 = ((bf16[16,2,3072]{2,1,0:T(2,128)(2,1)}), bf16[16,2,3072]{2,1,0:T(2,128)(2,1)S(1)}, u32[]{:S(2)}, u32[]{:S(2)}) async-start(bf16[16,2,3072]{2,1,0:T(2,128)(2,1)} %reshape.184), calls=%async_computation.2 | async-start | bytes 393216 | tf_op jit(solution)/shard_map/all_to_all | solution.py:32
  114.2 1.8 copy-start.4
  116.4 11.0 %copy-start.6 = (bf16[2,256,256]{2,1,0:T(8,128)(2,1)S(1)}, bf16[2,256,256]{2,1,0:T(8,128)(2,1)}, u32[]{:S(2)}) copy-start(bf16[2,256,256]{2,1,0:T(8,128)(2,1)} %param.18) | copy-start | bytes 786436
  119.8 16.3 %all-to-all-start.4 = ((bf16[16,2,3072]{2,1,0:T(2,128)(2,1)}), bf16[16,2,3072]{2,1,0:T(2,128)(2,1)}, u32[]{:S(2)}, u32[]{:S(2)}) async-start(bf16[16,2,3072]{2,1,0:T(2,128)(2,1)} %reshape.190), calls=%async_computation.4 | async-start | bytes 393216 | tf_op jit(solution)/shard_map/all_to_all | solution.py:38
  147.4 10.1 %copy-start.3 = (bf16[3,8,8,512]{3,2,1,0:T(8,128)(2,1)S(1)}, bf16[3,8,8,512]{3,2,1,0:T(8,128)(2,1)}, u32[]{:S(2)}) copy-start(bf16[3,8,8,512]{3,2,1,0:T(8,128)(2,1)} %param.14) | copy-start | bytes 589828
  150.7 26.5 %all-to-all-start.5 = ((bf16[32,2,1536]{2,1,0:T(2,128)(2,1)}), bf16[32,2,1536]{2,1,0:T(2,128)(2,1)S(1)}, u32[]{:S(2)}, u32[]{:S(2)}) async-start(bf16[32,2,1536]{2,1,0:T(2,128)(2,1)} %reshape.192), calls=%async_computation.5 | async-start | bytes 393216 | tf_op jit(solution)/shard_map/all_to_all | solution.py:40
where the time goes:
time: 270 us; the launch traced here: 268 us
  local copies, waits for them, and re-layouts  92.1 us (34%)
  blocking collectives  77.7 us (29%)
  starting transfers between devices  54.7 us (20%)
  waiting for transfers between devices  33.8 us (13%)
  other arithmetic  5.43 us (2%)
  matrix products  3.54 us (1%)
    psum x1, blocking collectives, on_device(): control_grad = lax.psum(span_local, 'col')  77.7 us
    unnamed x28, local copies, waits for them, and re-layouts  43.8 us
    all_to_all x1, waiting for transfers between devices, on_device(): lax.all_to_all(side_normal, 'row', split_axis=2, concat_axis=3, tiled=True)  19.1 us
    all_to_all x1, starting transfers between devices, on_device(): lax.all_to_all(velocity, 'row', split_axis=3, concat_axis=2, tiled=True)  18.2 us
    convert_element_type x3, local copies, waits for them, and re-layouts, on_device(): summed = part_x.astype(jnp.float32) + side_sum.astype(jnp.float32)  9.7 us
    all_to_all x2, local copies, waits for them, and re-layouts, on_device(): lax.all_to_all(adjoint, 'row', split_axis=3, concat_axis=2, tiled=True)  8.76 us
    all_to_all x3, local copies, waits for them, and re-layouts, on_device(): lax.all_to_all(velocity, 'row', split_axis=3, concat_axis=2, tiled=True)  8.46 us
    all_to_all x1, waiting for transfers between devices, on_device(): lax.all_to_all(velocity, 'row', split_axis=3, concat_axis=2, tiled=True)  8.4 us
  transfers between devices with their start and end apart: 6, of which 3 were waited for; matrix products, arithmetic and copies ran while one was open for 19% of the time, Pallas kernels for 0%

commit v1 on v0

--- a/solution.py
+++ b/solution.py
@@ -22,7 +22,7 @@
 def on_device(adjoint, velocity, control, deriv_x, deriv_y, deriv_z):
     part_x = directional(adjoint, velocity, deriv_x, 0, 3)
     span_local = jnp.sum(adjoint[0].astype(jnp.float32) * velocity[0].astype(jnp.float32), axis=0)
-    control_grad = lax.psum(span_local, "col")
+    control_grad = jnp.sum(lax.all_gather(span_local, "col"), axis=0)
     normal_adj, normal_vel = (
         lax.all_to_all(adjoint, "row", split_axis=3, concat_axis=2, tiled=True),
         lax.all_to_all(velocity, "row", split_axis=3, concat_axis=2, tiled=True),

time: 270 us -> 235 us (0.87)
  the two profiles are of different devices: /device:TPU:4 before, /device:TPU:6 now
where the time goes in v1:
time: 235 us; the launch traced here: 234 us
  local copies, waits for them, and re-layouts  92.1 us (39%)
  starting transfers between devices  54.4 us (23%)
  blocking collectives  42.4 us (18%)
  waiting for transfers between devices  34.1 us (15%)
  other arithmetic  6.05 us (3%)
  matrix products  3.54 us (2%)
    unnamed x28, local copies, waits for them, and re-layouts  43.8 us
    all_gather x1, blocking collectives, on_device(): control_grad = jnp.sum(lax.all_gather(span_local, 'col'), axis=0)  42.4 us
    all_to_all x1, waiting for transfers between devices, on_device(): lax.all_to_all(side_normal, 'row', split_axis=2, concat_axis=3, tiled=True)  19.1 us
    all_to_all x1, starting transfers between devices, on_device(): lax.all_to_all(velocity, 'row', split_axis=3, concat_axis=2, tiled=True)  18.2 us
    convert_element_type x3, local copies, waits for them, and re-layouts, on_device(): summed = part_x.astype(jnp.float32) + side_sum.astype(jnp.float32)  9.7 us
    all_to_all x2, local copies, waits for them, and re-layouts, on_device(): lax.all_to_all(adjoint, 'row', split_axis=3, concat_axis=2, tiled=True)  8.76 us
    all_to_all x3, local copies, waits for them, and re-layouts, on_device(): lax.all_to_all(velocity, 'row', split_axis=3, concat_axis=2, tiled=True)  8.46 us
    all_to_all x1, waiting for transfers between devices, on_device(): lax.all_to_all(velocity, 'row', split_axis=3, concat_axis=2, tiled=True)  8.38 us
  transfers between devices with their start and end apart: 6, of which 4 were waited for; matrix products, arithmetic and copies ran while one was open for 22% of the time, Pallas kernels for 0%

profile of v1, /device:TPU:6, one launch (start us, length us, event | category | flops | bytes accessed | tf_op | source)
XLA Modules:
  0.0 233.6 jit_solution(735528473565167458)
XLA Ops:
  0.6 4.4 %copy.73 = bf16[3,8,8,512]{2,1,0,3:T(8,128)(2,1)} copy(bf16[3,8,8,512]{3,2,1,0:T(8,128)(2,1)} %param.15) | data formatting | bytes 393216 | tf_op args[1]
  5.0 5.6 %reshape.187 = bf16[32,2,1536]{2,1,0:T(2,128)(2,1)} reshape(bf16[512,3,8,8]{3,2,1,0:T(8,128)(2,1)} %bitcast.132) | data formatting | bytes 393216
  10.7 18.2 %all-to-all-start.1 = ((bf16[32,2,1536]{2,1,0:T(2,128)(2,1)}), bf16[32,2,1536]{2,1,0:T(2,128)(2,1)S(1)}, u32[]{:S(2)}, u32[]{:S(2)}) async-start(bf16[32,2,1536]{2,1,0:T(2,128)(2,1)} %reshape.187), calls=%async_computation.1 | async-start | bytes 393216 | tf_op jit(solution)/shard_map/all_to_all | solution.py:28
  28.9 3.5 %copy.69 = bf16[3,8,8,512]{2,1,0,3:T(8,128)(2,1)} copy(bf16[3,8,8,512]{3,2,1,0:T(8,128)(2,1)S(1)} %copy-done.2) | data formatting | bytes 393216 | tf_op args[0]
  32.4 5.6 %reshape.183 = bf16[32,2,1536]{2,1,0:T(2,128)(2,1)} reshape(bf16[512,3,8,8]{3,2,1,0:T(8,128)(2,1)} %bitcast.133) | data formatting | bytes 393216
  38.0 8.4 %all-to-all-done.1 = bf16[32,2,1536]{2,1,0:T(2,128)(2,1)S(1)} async-done(((bf16[32,2,1536]{2,1,0:T(2,128)(2,1)}), bf16[32,2,1536]{2,1,0:T(2,128)(2,1)S(1)}, u32[]{:S(2)}, u32[]{:S(2)}) %all-to-all-start.1) | async-done | bytes 196640 | tf_op jit(solution)/shard_map/all_to_all | solution.py:28
  46.4 7.2 %all-to-all-start = ((bf16[32,2,1536]{2,1,0:T(2,128)(2,1)}), bf16[32,2,1536]{2,1,0:T(2,128)(2,1)S(1)}, u32[]{:S(2)}, u32[]{:S(2)}) async-start(bf16[32,2,1536]{2,1,0:T(2,128)(2,1)} %reshape.183), calls=%async_computation | async-start | bytes 393216 | tf_op jit(solution)/shard_map/all_to_all | solution.py:27
  53.6 4.8 %reshape.188 = bf16[512,3,8,8]{3,2,1,0:T(8,128)(2,1)} reshape(bf16[32,2,1536]{2,1,0:T(2,128)(2,1)S(1)} %all-to-all-done.1) | data formatting | bytes 393216
  58.3 4.0 %copy.101 = bf16[3,8,32,8,16]{4,1,0,3,2:T(8,128)(2,1)S(1)} copy(bf16[3,8,32,8,16]{3,1,0,4,2:T(8,128)(2,1)} %bitcast.124) | data formatting | bytes 393216 | tf_op jit(solution)/shard_map/all_to_all | solution.py:28
  62.3 2.3 %reshape.189 = bf16[16,2,3072]{2,1,0:T(2,128)(2,1)} reshape(bf16[256,3,8,16]{3,2,1,0:T(8,128)(2,1)S(1)} %bitcast.142) | data formatting | bytes 393216
  64.7 6.3 %all-to-all-done = bf16[32,2,1536]{2,1,0:T(2,128)(2,1)S(1)} async-done(((bf16[32,2,1536]{2,1,0:T(2,128)(2,1)}), bf16[32,2,1536]{2,1,0:T(2,128)(2,1)S(1)}, u32[]{:S(2)}, u32[]{:S(2)}) %all-to-all-start) | async-done | bytes 196640 | tf_op jit(solution)/shard_map/all_to_all | solution.py:27
  71.0 7.3 %all-to-all-start.3 = ((bf16[16,2,3072]{2,1,0:T(2,128)(2,1)}), bf16[16,2,3072]{2,1,0:T(2,128)(2,1)S(1)}, u32[]{:S(2)}, u32[]{:S(2)}) async-start(bf16[16,2,3072]{2,1,0:T(2,128)(2,1)} %reshape.189), calls=%async_computation.3 | async-start | bytes 393216 | tf_op jit(solution)/shard_map/all_to_all | solution.py:33
  78.3 4.8 %reshape.184 = bf16[512,3,8,8]{3,2,1,0:T(8,128)(2,1)} reshape(bf16[32,2,1536]{2,1,0:T(2,128)(2,1)S(1)} %all-to-all-done) | data formatting | bytes 393216
  83.1 4.0 %copy.100 = bf16[3,8,32,8,16]{4,1,0,3,2:T(8,128)(2,1)S(1)} copy(bf16[3,8,32,8,16]{3,1,0,4,2:T(8,128)(2,1)} %bitcast.126) | data formatting | bytes 393216 | tf_op jit(solution)/shard_map/all_to_all | solution.py:27
  87.1 2.3 %reshape.185 = bf16[16,2,3072]{2,1,0:T(2,128)(2,1)} reshape(bf16[256,3,8,16]{3,2,1,0:T(8,128)(2,1)S(1)} %bitcast.143) | data formatting | bytes 393216
  89.5 7.5 %all-to-all-start.2 = ((bf16[16,2,3072]{2,1,0:T(2,128)(2,1)}), bf16[16,2,3072]{2,1,0:T(2,128)(2,1)S(1)}, u32[]{:S(2)}, u32[]{:S(2)}) async-start(bf16[16,2,3072]{2,1,0:T(2,128)(2,1)} %reshape.185), calls=%async_computation.2 | async-start | bytes 393216 | tf_op jit(solution)/shard_map/all_to_all | solution.py:32
  97.1 4.8 %copy.71 = bf16[3,8,32,8,16]{4,3,2,1,0:T(8,128)(2,1)} copy(bf16[3,8,32,8,16]{3,1,0,4,2:T(8,128)(2,1)} %bitcast.127) | data formatting | bytes 393216 | tf_op jit(solution)/shard_map/all_to_all | solution.py:27
  105.1 2.1 copy.103
  111.8 2.3 copy.83
  117.4 2.3 %reshape.191 = bf16[16,2,3072]{2,1,0:T(2,128)(2,1)} reshape(bf16[128,3,16,16]{3,2,1,0:T(8,128)(2,1)S(1)} %bitcast.136) | data formatting | bytes 393216
  119.7 7.6 %all-to-all-start.4 = ((bf16[16,2,3072]{2,1,0:T(2,128)(2,1)}), bf16[16,2,3072]{2,1,0:T(2,128)(2,1)}, u32[]{:S(2)}, u32[]{:S(2)}) async-start(bf16[16,2,3072]{2,1,0:T(2,128)(2,1)} %reshape.191), calls=%async_computation.4 | async-start | bytes 393216 | tf_op jit(solution)/shard_map/all_to_all | solution.py:38
  127.3 2.9 %fusion.2 = f32[2,3,8,256,16]{3,4,2,1,0:T(8,128)} fusion(bf16[3,8,32,8,16]{4,3,2,1,0:T(8,128)(2,1)} %copy.71, bf16[2,256,256]{2,1,0:T(8,128)(2,1)S(1)} %copy-done.6), kind=kOutput, calls=%fused_computation.3 | convolution fusion | flops 100663296 | bytes 1245184 | tf_op jit(solution)/shard_map/abpd,mpq->mabqd/dot_general | solution.py:11
  130.2 3.9 %copy.75 = bf16[3,8,32,8,16]{4,3,2,1,0:T(8,128)(2,1)S(1)} copy(bf16[3,8,32,8,16]{3,1,0,4,2:T(8,128)(2,1)} %bitcast.125) | data formatting | bytes 393216 | tf_op jit(solution)/shard_map/all_to_all | solution.py:28
  136.3 2.3 reshape.192
  140.9 3.7 %copy.86 = f32[3,8,16,16,16]{3,2,4,1,0:T(8,128)} copy(f32[3,8,16,16,16]{4,3,1,2,0:T(8,128)} %convert_bitcast_fusion) | data formatting | bytes 786432 | tf_op jit(solution)/shard_map/convert_element_type | solution.py:39
  144.7 2.8 %reshape.171 = f32[3,8,256,16]{2,3,1,0:T(8,128)S(1)} reshape(f32[3,8,16,16,16]{3,2,4,1,0:T(8,128)} %copy.86) | data formatting | bytes 786432 | tf_op jit(solution)/shard_map/convert_element_type | solution.py:39
  148.5 2.4 %reshape.193 = bf16[32,2,1536]{2,1,0:T(2,128)(2,1)} reshape(bf16[256,3,8,16]{3,2,1,0:T(8,128)(2,1)S(1)} %bitcast.138) | data formatting | bytes 393216
  150.8 6.7 %all-to-all-start.5 = ((bf16[32,2,1536]{2,1,0:T(2,128)(2,1)}), bf16[32,2,1536]{2,1,0:T(2,128)(2,1)S(1)}, u32[]{:S(2)}, u32[]{:S(2)}) async-start(bf16[32,2,1536]{2,1,0:T(2,128)(2,1)} %reshape.193), calls=%async_computation.5 | async-start | bytes 393216 | tf_op jit(solution)/shard_map/all_to_all | solution.py:40
  158.0 19.1 %all-to-all-done.5 = bf16[32,2,1536]{2,1,0:T(2,128)(2,1)S(1)} async-done(((bf16[32,2,1536]{2,1,0:T(2,128)(2,1)}), bf16[32,2,1536]{2,1,0:T(2,128)(2,1)S(1)}, u32[]{:S(2)}, u32[]{:S(2)}) %all-to-all-start.5) | async-done | bytes 196640 | tf_op jit(solution)/shard_map/all_to_all | solution.py:40
  181.1 4.1 %copy.90 = f32[3,8,8,32,16]{4,3,2,1,0:T(8,128)} copy(f32[3,8,8,32,16]{4,2,3,1,0:T(8,128)} %bitcast.131) | data formatting | bytes 786432 | tf_op jit(solution)/shard_map/convert_element_type | solution.py:41
  185.3 3.6 %reshape.172 = f32[3,8,8,512]{3,2,1,0:T(8,128)S(1)} reshape(f32[3,8,8,32,16]{4,3,2,1,0:T(8,128)} %copy.90) | data formatting | bytes 786432 | tf_op jit(solution)/shard_map/convert_element_type | solution.py:41
  190.6 42.4 %all-gather = f32[128,512]{1,0:T(8,128)S(1)} all-gather(f32[8,512]{1,0:T(8,128)S(1)} %get-tuple-element.56), channel_id=2, replica_groups=mesh['row'=32,'col'=16] {'col'}, dimensions={0}, use_global_device_ids=true | all-gather | bytes 278528 | tf_op jit(solution)/shard_map/all_gather | solution.py:25
  (51 shorter events, 23.3 us)
Async XLA Ops:
  0.6 156.9 %copy-start = (bf16[2,512,512]{2,1,0:T(8,128)(2,1)S(1)}, bf16[2,512,512]{2,1,0:T(8,128)(2,1)}, u32[]{:S(2)}) copy-start(bf16[2,512,512]{2,1,0:T(8,128)(2,1)} %param.17) | copy-start | bytes 3145732
  5.0 23.8 %copy-start.2 = (bf16[3,8,8,512]{3,2,1,0:T(8,128)(2,1)S(1)}, bf16[3,8,8,512]{3,2,1,0:T(8,128)(2,1)}, u32[]{:S(2)}) copy-start(bf16[3,8,8,512]{3,2,1,0:T(8,128)(2,1)} %param.14) | copy-start | bytes 589828
  10.7 35.7 %all-to-all-start.1 = ((bf16[32,2,1536]{2,1,0:T(2,128)(2,1)}), bf16[32,2,1536]{2,1,0:T(2,128)(2,1)S(1)}, u32[]{:S(2)}, u32[]{:S(2)}) async-start(bf16[32,2,1536]{2,1,0:T(2,128)(2,1)} %reshape.187), calls=%async_computation.1 | async-start | bytes 393216 | tf_op jit(solution)/shard_map/all_to_all | solution.py:28
  46.4 24.6 %all-to-all-start = ((bf16[32,2,1536]{2,1,0:T(2,128)(2,1)}), bf16[32,2,1536]{2,1,0:T(2,128)(2,1)S(1)}, u32[]{:S(2)}, u32[]{:S(2)}) async-start(bf16[32,2,1536]{2,1,0:T(2,128)(2,1)} %reshape.183), calls=%async_computation | async-start | bytes 393216 | tf_op jit(solution)/shard_map/all_to_all | solution.py:27
  71.0 18.5 %all-to-all-start.3 = ((bf16[16,2,3072]{2,1,0:T(2,128)(2,1)}), bf16[16,2,3072]{2,1,0:T(2,128)(2,1)S(1)}, u32[]{:S(2)}, u32[]{:S(2)}) async-start(bf16[16,2,3072]{2,1,0:T(2,128)(2,1)} %reshape.189), calls=%async_computation.3 | async-start | bytes 393216 | tf_op jit(solution)/shard_map/all_to_all | solution.py:33
  87.1 9.9 %copy-start.1 = (bf16[3,8,8,512]{3,2,1,0:T(8,128)(2,1)S(1)}, bf16[3,8,8,512]{3,2,1,0:T(8,128)(2,1)}, u32[]{:S(2)}) copy-start(bf16[3,8,8,512]{3,2,1,0:T(8,128)(2,1)} %param.15) | copy-start | bytes 589828
  87.1 9.9 %copy-start.5 = (bf16[8,512]{1,0:T(8,128)(2,1)S(1)}, bf16[8,512]{1,0:T(8,128)(2,1)}, u32[]{:S(2)}) copy-start(bf16[8,512]{1,0:T(8,128)(2,1)} %param.16) | copy-start | bytes 24580
  89.5 17.8 %all-to-all-start.2 = ((bf16[16,2,3072]{2,1,0:T(2,128)(2,1)}), bf16[16,2,3072]{2,1,0:T(2,128)(2,1)S(1)}, u32[]{:S(2)}, u32[]{:S(2)}) async-start(bf16[16,2,3072]{2,1,0:T(2,128)(2,1)} %reshape.185), calls=%async_computation.2 | async-start | bytes 393216 | tf_op jit(solution)/shard_map/all_to_all | solution.py:32
  114.1 1.8 copy-start.4
  116.3 11.0 %copy-start.6 = (bf16[2,256,256]{2,1,0:T(8,128)(2,1)S(1)}, bf16[2,256,256]{2,1,0:T(8,128)(2,1)}, u32[]{:S(2)}) copy-start(bf16[2,256,256]{2,1,0:T(8,128)(2,1)} %param.18) | copy-start | bytes 786436
  119.7 16.6 %all-to-all-start.4 = ((bf16[16,2,3072]{2,1,0:T(2,128)(2,1)}), bf16[16,2,3072]{2,1,0:T(2,128)(2,1)}, u32[]{:S(2)}, u32[]{:S(2)}) async-start(bf16[16,2,3072]{2,1,0:T(2,128)(2,1)} %reshape.191), calls=%async_computation.4 | async-start | bytes 393216 | tf_op jit(solution)/shard_map/all_to_all | solution.py:38
  147.5 10.0 %copy-start.3 = (bf16[3,8,8,512]{3,2,1,0:T(8,128)(2,1)S(1)}, bf16[3,8,8,512]{3,2,1,0:T(8,128)(2,1)}, u32[]{:S(2)}) copy-start(bf16[3,8,8,512]{3,2,1,0:T(8,128)(2,1)} %param.14) | copy-start | bytes 589828
  150.8 26.4 %all-to-all-start.5 = ((bf16[32,2,1536]{2,1,0:T(2,128)(2,1)}), bf16[32,2,1536]{2,1,0:T(2,128)(2,1)S(1)}, u32[]{:S(2)}, u32[]{:S(2)}) async-start(bf16[32,2,1536]{2,1,0:T(2,128)(2,1)} %reshape.193), calls=%async_computation.5 | async-start | bytes 393216 | tf_op jit(solution)/shard_map/all_to_all | solution.py:40
